TPU v7x, 32 devices: a whole 2x2x4 slice. The times are simulated.
32 devices in a mesh: row: 8 (over y, x, core), col: 4 (over z).
Axes of the slice: x: 2, y: 2, z: 4, core: 2. Of those that a mesh axis runs over, the one named last changes fastest.
Arguments:
- amplitudes: bfloat16 [4096, 4096], P('row', 'col'), may hold values from -0.1875 to 0.1875
- factors: bfloat16 [4096, 2048], P('col', 'row'), may hold values from -0.125 to 0.125
- tile_map: int32 [16, 16], P('row', 'col'), may hold values 0 or 1
- panel_owner: int32 [2], replicated, may hold values from 0 to 3, as said below
Outputs:
- cycle_term: float32 [4096, 4096], P('row', 'col')
Inputs may be any that keep to these rules, and one draw needn't show every extreme that they name: `panel_owner`: the 2 entries are distinct panel indices, and one of them is the last panel.
All inputs are finite; a program needn't handle non-finite values. No bound on the sum of `tile_map` on one device may be relied on, other than what follows from the above.
Results may differ from a plain program's by a relative error of at most 0.0029.
Values may be sent and summed in bfloat16 or wider, within the bound.
A program may use at most 64 MiB of HBM per device.

v0:
```python
import jax
import jax.numpy as jnp
from jax import lax
from jax.sharding import PartitionSpec as P


def spread(block, axis, owner):
    block = jnp.where(lax.axis_index(axis) == owner, block, jnp.zeros_like(block))
    return lax.psum(block, axis)


def keep_tiles(block, tiles):
    rows, cols = tiles.shape
    shaped = block.reshape(rows, block.shape[0] // rows, cols, block.shape[1] // cols)
    keep = tiles.astype(block.dtype)[:, None, :, None]
    return (shaped * keep).reshape(block.shape)


def outer_rows(left, right):
    return lax.dot_general(
        left, right, (((1,), (1,)), ((), ())), preferred_element_type=jnp.float32
    )


def shards(amplitudes, factors, tile_map, panel_owner):
    kept = keep_tiles(amplitudes, tile_map)
    width = factors.shape[0]
    total = jnp.zeros((kept.shape[0], width), jnp.float32)
    column_factors = lax.all_gather(factors, "row", axis=1, tiled=True)
    for step in range(panel_owner.shape[0]):
        owner = panel_owner[step]
        panel = spread(kept, "col", owner)
        owner_slice = spread(factors, "col", owner)
        owner_factors = lax.all_gather(owner_slice, "row", axis=1, tiled=True)
        integrals = outer_rows(owner_factors, column_factors).astype(jnp.bfloat16)
        total = total + jnp.dot(panel, integrals, preferred_element_type=jnp.float32)
    return keep_tiles(total, tile_map)


def solution(mesh):
    in_specs = (P("row", "col"), P("col", "row"), P("row", "col"), P())
    out_specs = P("row", "col")
    return jax.shard_map(shards, mesh=mesh, in_specs=in_specs, out_specs=out_specs, check_vma=False)
```

profile of v0, /device:TPU:0, one launch (start us, length us, event | category | flops | bytes accessed | tf_op | source)
XLA Modules:
  0.0 232.9 jit_solution(12405336362898462879)
XLA Ops:
  7.4 0.0 all-reduce.3.cloned.1.call-start
  7.4 0.8 fusion.10
  8.2 1.3 fusion.11
  9.4 0.3 mul.22
  9.8 0.2 copy.5
  11.2 2.1 broadcast_select_fusion.3
  13.3 0.0 copy-done
  13.3 1.5 broadcast_select_fusion.1
  14.8 0.0 all-reduce.3.cloned.1.call-update
  14.9 0.0 all-gather.6.cloned.1.call-start
  14.9 0.5 all-gather.6.cloned.1.call-update
  15.4 0.0 all-gather.8.cloned.1.call-start
  15.5 123.3 %all-reduce.3.cloned.1.call-done = (bf16[512,1024]{1,0:T(8,128)(2,1)}, bf16[1024,256]{1,0:T(8,128)(2,1)}, bf16[512,1024]{1,0:T(8,128)(2,1)}, bf16[1024,256]{1,0:T(8,128)(2,1)}) async-done(((bf16[512,1024]{1,0:T(8,128)(2,1)}, bf16[1024,256]{1,0:T(8,128)(2,1)}, bf16[512,1024]{1,0:T(8,128)(2,1)}, bf16[1024,256]{1,0:T(8,128)(2,1)}), (bf16[512,1024]{1,0:T(8,128)(2,1)}, bf16[1024,256]{1,0:T(8,128)(2,1)}, ...) | async-done | bytes 3145744 | tf_op jit(solution)/shard_map/psum | solution.py:9
  138.8 0.0 all-gather.8.cloned.1.call-update
  138.9 0.0 all-gather.4.cloned.1.call-start
  138.9 0.5 all-gather.4.cloned.1.call-update
  139.4 0.3 mul.25
  139.8 0.5 copy.6
  140.3 0.0 all-gather.6.cloned.1.call-done
  140.3 34.9 %all-gather.8.cloned.1.call-done = bf16[1024,2048]{1,0:T(8,128)(2,1)} async-done(((bf16[1024,256]{1,0:T(8,128)(2,1)}), bf16[1024,2048]{1,0:T(8,128)(2,1)}) %all-gather.8.cloned.1.call-update) | async-done | bytes 4194320 | tf_op jit(solution)/shard_map/all_gather | solution.py:34
  175.2 10.8 %fusion = f32[512,1024]{1,0:T(8,128)} fusion(bf16[512,1024]{1,0:T(8,128)(2,1)} %get-tuple-element.5, bf16[1024,2048]{1,0:T(8,128)(2,1)} %all-gather.8.cloned.1.call-done, bf16[1024,2048]{1,0:T(8,128)(2,1)} %all-gather.6.cloned.1.call-done), kind=kOutput, calls=%fused_computation.1 | convolution fusion | flops 5369757696 | bytes 11534336 | tf_op jit(solution)/shard_map/dot_general | solution.py:36
  186.0 28.2 %all-gather.4.cloned.1.call-done = bf16[1024,2048]{1,0:T(8,128)(2,1)} async-done(((bf16[1024,256]{1,0:T(8,128)(2,1)}), bf16[1024,2048]{1,0:T(8,128)(2,1)}) %all-gather.4.cloned.1.call-update) | async-done | bytes 4194320 | tf_op jit(solution)/shard_map/all_gather | solution.py:34
  214.2 0.0 copy-done.1
  214.2 11.1 %add_multiply_fusion = f32[512,1024]{1,0:T(8,128)} fusion(f32[512,1024]{1,0:T(8,128)S(1)} %bitcast.17, f32[512,1024]{1,0:T(8,128)} %fusion, bf16[512,1024]{1,0:T(8,128)(2,1)S(1)} %copy-done.1, bf16[1024,2048]{1,0:T(8,128)(2,1)} %all-gather.4.cloned.1.call-done, bf16[1024,2048]{1,0:T(8,128)(2,1)} %all-gather.6.cloned.1.call-done), kind=kOutput, calls=%fused_computation | convolution fusion | flops 5370806272 | bytes 15728640 | tf_op jit(solution)/shard_map/dot_general | solution.py:36
  (2 shorter events, 0.0 us)
Async XLA Ops:
  7.4 6.0 %copy-start = (bf16[512,1024]{1,0:T(8,128)(2,1)S(1)}, bf16[512,1024]{1,0:T(8,128)(2,1)}, u32[]{:S(2)}) copy-start(bf16[512,1024]{1,0:T(8,128)(2,1)} %param.4) | copy-start | bytes 3145732
  7.4 131.5 %all-reduce.3.cloned.1.call-start = ((), (), s32[]{:S(2)}) async-start(), calls=%async_computation.3 | async-start | bytes 6291456 | tf_op jit(solution)/shard_map/psum | solution.py:9
  14.9 125.4 %all-gather.6.cloned.1.call-start = ((), (), s32[]{:S(2)}) async-start(), calls=%async_computation.1 | async-start | bytes 4718592 | tf_op jit(solution)/shard_map/all_gather | solution.py:29
  15.4 159.8 %all-gather.8.cloned.1.call-start = ((), (), s32[]{:S(2)}) async-start(), calls=%async_computation.2 | async-start | bytes 4718592 | tf_op jit(solution)/shard_map/all_gather | solution.py:34
  138.9 75.3 %all-gather.4.cloned.1.call-start = ((), (), s32[]{:S(2)}) async-start(), calls=%async_computation | async-start | bytes 4718592 | tf_op jit(solution)/shard_map/all_gather | solution.py:34
  175.2 39.0 %copy-start.1 = (bf16[512,1024]{1,0:T(8,128)(2,1)S(1)}, bf16[512,1024]{1,0:T(8,128)(2,1)}, u32[]{:S(2)}) copy-start(bf16[512,1024]{1,0:T(8,128)(2,1)} %get-tuple-element.7) | copy-start | bytes 3145732
Sparse Core Ops, SparseCore 0:
  15.0 123.8 all-reduce.2
Sparse Core Ops, SparseCore 1:
  17.2 39.9 all-gather.5
  139.0 36.2 all-gather.7
  177.0 37.2 all-gather.3
where the time goes:
time: 233 us
  waiting for transfers between devices  188 us (81%)
  matrix products  21.9 us (9%)
  between operations  16.3 us (7%)
  other arithmetic  4.41 us (2%)
  local copies, waits for them, and re-layouts  2.65 us (1%)
    psum x1, waiting for transfers between devices, spread(): return lax.psum(block, axis)  123 us
    all_gather x2, waiting for transfers between devices, shards(): owner_factors = lax.all_gather(owner_slice, 'row', axis=1, tiled=True)  63.1 us
    dot_general x2, matrix products, shards(): jnp.dot(panel, integrals, preferred_element_type=jnp.float32)  21.9 us
  transfers between devices with their start and end apart: 4, of which 3 were waited for; matrix products, arithmetic and copies ran while one was open for 5% of the time, Pallas kernels for 0%

commit v1 on v0

--- a/solution.py
+++ b/solution.py
@@ -2,6 +2,24 @@
 import jax.numpy as jnp
 from jax import lax
 from jax.sharding import PartitionSpec as P
+
+
+def _measure_face(w_in):
+    top, frame_out, x_new = (lax.axis_size("row"), lax.axis_index("row"), w_in.shape[1])
+    opened = lax.dynamic_update_slice_in_dim(
+        jnp.zeros(
+            tuple((k0 * top if j0 == 1 else k0 for j0, k0 in enumerate(w_in.shape))), w_in.dtype
+        ),
+        w_in,
+        frame_out * x_new,
+        axis=1,
+    )
+    for c in tuple(range(1, top)):
+        w_in = lax.ppermute(w_in, "row", tuple(((j0, (j0 + 1) % top) for j0 in range(top))))
+        opened = lax.dynamic_update_slice_in_dim(
+            opened, w_in, (frame_out - c) % top * x_new, axis=1
+        )
+    return opened
 
 
 def spread(block, axis, owner):
@@ -31,7 +49,7 @@
         owner = panel_owner[step]
         panel = spread(kept, "col", owner)
         owner_slice = spread(factors, "col", owner)
-        owner_factors = lax.all_gather(owner_slice, "row", axis=1, tiled=True)
+        owner_factors = _measure_face(owner_slice)
         integrals = outer_rows(owner_factors, column_factors).astype(jnp.bfloat16)
         total = total + jnp.dot(panel, integrals, preferred_element_type=jnp.float32)
     return keep_tiles(total, tile_map)

time: 233 us -> 254 us (1.090)
  local copies, waits for them, and re-layouts: 2.65 us -> 26 us
  waiting for transfers between devices: 188 us -> 183 us
    all_gather x2 -> x0, waiting for transfers between devices: 63.1 us -> none  [shards(): owner_factors = lax.all_gather(owner_slice, 'row', axis=1, tiled=True)]
    ppermute x0 -> x14, waiting for transfers between devices: none -> 58.8 us  [_measure_face(): lax.ppermute(w_in, 'row', tuple(((j0, (j0 + 1) % top) for j0 in range(top...]
    dynamic_update_slice x0 -> x16, local copies, waits for them, and re-layouts: none -> 18.2 us  [the longest x14 16.4 us: _measure_face(): lax.dynamic_update_slice_in_dim(opened, w_in, (frame_out - c) % top * x_n...]
    another operation x0 -> x2, local copies, waits for them, and re-layouts: none -> 5.07 us
  transfers between devices with their start and end apart: 4 -> 16, of which waited for: 3 -> 14; matrix products, arithmetic and copies ran while one was open for 5% -> 9% of each run, Pallas kernels for 0% -> 0%
where the time goes in v1:
time: 254 us
  waiting for transfers between devices  183 us (72%)
  local copies, waits for them, and re-layouts  26 us (10%)
  matrix products  22.1 us (9%)
  between operations  16.2 us (6%)
  other arithmetic  4.42 us (2%)
    psum x1, waiting for transfers between devices, spread(): return lax.psum(block, axis)  123 us
    ppermute x14, waiting for transfers between devices, _measure_face(): lax.ppermute(w_in, 'row', tuple(((j0, (j0 + 1) % top) for j0 in range(top...  58.8 us
    dot_general x2, matrix products, shards(): jnp.dot(panel, integrals, preferred_element_type=jnp.float32)  22.1 us
    dynamic_update_slice x14, local copies, waits for them, and re-layouts, _measure_face(): lax.dynamic_update_slice_in_dim(opened, w_in, (frame_out - c) % top * x_n...  16.4 us
  transfers between devices with their start and end apart: 16, of which 14 were waited for; matrix products, arithmetic and copies ran while one was open for 9% of the time, Pallas kernels for 0%

profile of v1, /device:TPU:0, one launch (start us, length us, event | category | flops | bytes accessed | tf_op | source)
XLA Modules:
  0.0 253.8 jit_solution(10970468050443487904)
XLA Ops:
  7.4 1.4 fusion.11
  11.3 2.1 broadcast_select_fusion.3
  13.4 1.6 broadcast_select_fusion.1
  15.6 123.4 %all-reduce.3.cloned.1.call-done = (bf16[512,1024]{1,0:T(8,128)(2,1)}, bf16[1024,256]{1,0:T(8,128)(2,1)}, bf16[512,1024]{1,0:T(8,128)(2,1)}, bf16[1024,256]{1,0:T(8,128)(2,1)}) async-done(((bf16[512,1024]{1,0:T(8,128)(2,1)}, bf16[1024,256]{1,0:T(8,128)(2,1)}, bf16[512,1024]{1,0:T(8,128)(2,1)}, bf16[1024,256]{1,0:T(8,128)(2,1)}), (bf16[512,1024]{1,0:T(8,128)(2,1)}, bf16[1024,256]{1,0:T(8,128)(2,1)}, ...) | async-done | bytes 3145744 | tf_op jit(solution)/shard_map/psum | solution.py:27
  139.0 1.6 collective-permute-start.7
  140.6 8.1 %collective-permute-done = bf16[1024,256]{1,0:T(8,128)(2,1)S(1)} collective-permute-done((bf16[1024,256]{1,0:T(8,128)(2,1)}, bf16[1024,256]{1,0:T(8,128)(2,1)S(1)}, u32[]{:S(2)}, u32[]{:S(2)}) %collective-permute-start) | collective-permute-done | bytes 524320 | tf_op jit(solution)/shard_map/ppermute | solution.py:18
  148.7 5.6 %collective-permute-done.7 = bf16[1024,256]{1,0:T(8,128)(2,1)S(1)} collective-permute-done((bf16[1024,256]{1,0:T(8,128)(2,1)}, bf16[1024,256]{1,0:T(8,128)(2,1)S(1)}, u32[]{:S(2)}, u32[]{:S(2)}) %collective-permute-start.7) | collective-permute-done | bytes 524320 | tf_op jit(solution)/shard_map/ppermute | solution.py:18
  154.3 5.6 %collective-permute-done.1 = bf16[1024,256]{1,0:T(8,128)(2,1)S(1)} collective-permute-done((bf16[1024,256]{1,0:T(8,128)(2,1)S(1)}, bf16[1024,256]{1,0:T(8,128)(2,1)S(1)}, u32[]{:S(2)}, u32[]{:S(2)}) %collective-permute-start.1) | collective-permute-done | bytes 524320 | tf_op jit(solution)/shard_map/ppermute | solution.py:18
  160.0 5.6 %collective-permute-done.8 = bf16[1024,256]{1,0:T(8,128)(2,1)S(1)} collective-permute-done((bf16[1024,256]{1,0:T(8,128)(2,1)S(1)}, bf16[1024,256]{1,0:T(8,128)(2,1)S(1)}, u32[]{:S(2)}, u32[]{:S(2)}) %collective-permute-start.8) | collective-permute-done | bytes 524320 | tf_op jit(solution)/shard_map/ppermute | solution.py:18
  165.6 5.6 %collective-permute-done.2 = bf16[1024,256]{1,0:T(8,128)(2,1)S(1)} collective-permute-done((bf16[1024,256]{1,0:T(8,128)(2,1)S(1)}, bf16[1024,256]{1,0:T(8,128)(2,1)S(1)}, u32[]{:S(2)}, u32[]{:S(2)}) %collective-permute-start.2) | collective-permute-done | bytes 524320 | tf_op jit(solution)/shard_map/ppermute | solution.py:18
  171.2 5.7 %collective-permute-done.9 = bf16[1024,256]{1,0:T(8,128)(2,1)} collective-permute-done((bf16[1024,256]{1,0:T(8,128)(2,1)S(1)}, bf16[1024,256]{1,0:T(8,128)(2,1)}, u32[]{:S(2)}, u32[]{:S(2)}) %collective-permute-start.9) | collective-permute-done | bytes 524320 | tf_op jit(solution)/shard_map/ppermute | solution.py:18
  176.9 5.6 %collective-permute-done.3 = bf16[1024,256]{1,0:T(8,128)(2,1)} collective-permute-done((bf16[1024,256]{1,0:T(8,128)(2,1)S(1)}, bf16[1024,256]{1,0:T(8,128)(2,1)}, u32[]{:S(2)}, u32[]{:S(2)}) %collective-permute-start.3) | collective-permute-done | bytes 524320 | tf_op jit(solution)/shard_map/ppermute | solution.py:18
  183.4 4.7 %collective-permute-done.10 = bf16[1024,256]{1,0:T(8,128)(2,1)} collective-permute-done((bf16[1024,256]{1,0:T(8,128)(2,1)}, bf16[1024,256]{1,0:T(8,128)(2,1)}, u32[]{:S(2)}, u32[]{:S(2)}) %collective-permute-start.10) | collective-permute-done | bytes 524320 | tf_op jit(solution)/shard_map/ppermute | solution.py:18
  188.2 2.5 broadcast.21.clone.1
  191.6 2.5 %broadcast.21.clone = bf16[1024,2048]{1,0:T(8,128)(2,1)} broadcast(bf16[]{:T(256)} %constant.75.clone.1), dimensions={} | broadcast | bytes 4194306 | tf_op jit(solution)/shard_map/broadcast.3
  201.0 1.9 constant_dynamic-update-slice_fusion.4
  202.9 1.9 constant_dynamic-update-slice_fusion.11
  204.8 1.7 collective-permute-done.5
  206.5 1.9 constant_dynamic-update-slice_fusion.3
  208.4 3.7 %collective-permute-done.12 = bf16[1024,256]{1,0:T(8,128)(2,1)S(1)} collective-permute-done((bf16[1024,256]{1,0:T(8,128)(2,1)S(1)}, bf16[1024,256]{1,0:T(8,128)(2,1)S(1)}, u32[]{:S(2)}, u32[]{:S(2)}) %collective-permute-start.12) | collective-permute-done | bytes 524320 | tf_op jit(solution)/shard_map/ppermute | solution.py:18
  212.1 1.9 constant_dynamic-update-slice_fusion.10
  218.6 4.7 %collective-permute-done.13 = bf16[1024,256]{1,0:T(8,128)(2,1)S(1)} collective-permute-done((bf16[1024,256]{1,0:T(8,128)(2,1)S(1)}, bf16[1024,256]{1,0:T(8,128)(2,1)S(1)}, u32[]{:S(2)}, u32[]{:S(2)}) %collective-permute-start.13) | collective-permute-done | bytes 524320 | tf_op jit(solution)/shard_map/ppermute | solution.py:18
  224.2 10.7 %fusion = f32[512,1024]{1,0:T(8,128)} fusion(bf16[512,1024]{1,0:T(8,128)(2,1)} %get-tuple-element.5, bf16[1024,2048]{1,0:T(8,128)(2,1)} %constant_dynamic-update-slice_fusion, bf16[1024,2048]{1,0:T(8,128)(2,1)} %all-gather.2.cloned.1.call-done), kind=kOutput, calls=%fused_computation.1 | convolution fusion | flops 5369757696 | bytes 11534336 | tf_op jit(solution)/shard_map/dot_general | solution.py:54
  234.9 11.4 %add_multiply_fusion = f32[512,1024]{1,0:T(8,128)} fusion(f32[512,1024]{1,0:T(8,128)S(1)} %bitcast.17, f32[512,1024]{1,0:T(8,128)} %fusion, bf16[512,1024]{1,0:T(8,128)(2,1)} %get-tuple-element.7, bf16[1024,2048]{1,0:T(8,128)(2,1)} %constant_dynamic-update-slice_fusion.8, bf16[1024,2048]{1,0:T(8,128)(2,1)} %all-gather.2.cloned.1.call-done), kind=kOutput, calls=%fused_computation | convolution fusion | flops 5370806272 | bytes 15728640 | tf_op jit(solution)/shard_map/dot_general | solution.py:54
  (60 shorter events, 16.0 us)
Async XLA Ops:
  7.4 6.1 %copy-start = (bf16[512,1024]{1,0:T(8,128)(2,1)S(1)}, bf16[512,1024]{1,0:T(8,128)(2,1)}, u32[]{:S(2)}) copy-start(bf16[512,1024]{1,0:T(8,128)(2,1)} %param.4) | copy-start | bytes 3145732
  7.4 131.6 %all-reduce.3.cloned.1.call-start = ((), (), s32[]{:S(2)}) async-start(), calls=%async_computation.1 | async-start | bytes 6291456 | tf_op jit(solution)/shard_map/psum | solution.py:27
  15.0 209.2 %all-gather.2.cloned.1.call-start = ((), (), s32[]{:S(2)}) async-start(), calls=%async_computation | async-start | bytes 4718592 | tf_op jit(solution)/shard_map/all_gather | solution.py:47
  139.0 9.7 %collective-permute-start = (bf16[1024,256]{1,0:T(8,128)(2,1)}, bf16[1024,256]{1,0:T(8,128)(2,1)S(1)}, u32[]{:S(2)}, u32[]{:S(2)}) collective-permute-start(bf16[1024,256]{1,0:T(8,128)(2,1)} %get-tuple-element.8), channel_id=1, source_target_pairs={{0,4},{4,8},{8,12},{12,16},{16,20},{20,24},{24,28},{28,0},{1,5},{5... | collective-permute-start | bytes 1572872 | tf_op jit(solution)/shard_map/ppermute | solution.py:18
  139.0 15.3 %collective-permute-start.7 = (bf16[1024,256]{1,0:T(8,128)(2,1)}, bf16[1024,256]{1,0:T(8,128)(2,1)S(1)}, u32[]{:S(2)}, u32[]{:S(2)}) collective-permute-start(bf16[1024,256]{1,0:T(8,128)(2,1)} %get-tuple-element.6), channel_id=1, source_target_pairs={{0,4},{4,8},{8,12},{12,16},{16,20},{20,24},{24,28},{28,0},{1,5},{5... | collective-permute-start | bytes 1572872 | tf_op jit(solution)/shard_map/ppermute | solution.py:18
  148.7 11.2 %collective-permute-start.1 = (bf16[1024,256]{1,0:T(8,128)(2,1)S(1)}, bf16[1024,256]{1,0:T(8,128)(2,1)S(1)}, u32[]{:S(2)}, u32[]{:S(2)}) collective-permute-start(bf16[1024,256]{1,0:T(8,128)(2,1)S(1)} %collective-permute-done), channel_id=1, source_target_pairs={{0,4},{4,8},{8,12},{12,16},{16,20},{20,24},{24,28},{28,0},{1,5},{5... | collective-permute-start | bytes 1572872 | tf_op jit(solution)/shard_map/ppermute | solution.py:18
  154.3 28.2 %copy-start.9 = (bf16[1024,256]{1,0:T(8,128)(2,1)}, bf16[1024,256]{1,0:T(8,128)(2,1)S(1)}, u32[]{:S(2)}) copy-start(bf16[1024,256]{1,0:T(8,128)(2,1)S(1)} %collective-permute-done.7) | copy-start | bytes 1572868
  154.3 11.2 %collective-permute-start.8 = (bf16[1024,256]{1,0:T(8,128)(2,1)S(1)}, bf16[1024,256]{1,0:T(8,128)(2,1)S(1)}, u32[]{:S(2)}, u32[]{:S(2)}) collective-permute-start(bf16[1024,256]{1,0:T(8,128)(2,1)S(1)} %collective-permute-done.7), channel_id=1, source_target_pairs={{0,4},{4,8},{8,12},{12,16},{16,20},{20,24},{24,28},{28,0},{1,5},{5... | collective-permute-start | bytes 1572872 | tf_op jit(solution)/shard_map/ppermute | solution.py:18
  160.0 17.0 %copy-start.3 = (bf16[1024,256]{1,0:T(8,128)(2,1)}, bf16[1024,256]{1,0:T(8,128)(2,1)S(1)}, u32[]{:S(2)}) copy-start(bf16[1024,256]{1,0:T(8,128)(2,1)S(1)} %collective-permute-done.1) | copy-start | bytes 1572868
  160.0 11.2 %collective-permute-start.2 = (bf16[1024,256]{1,0:T(8,128)(2,1)S(1)}, bf16[1024,256]{1,0:T(8,128)(2,1)S(1)}, u32[]{:S(2)}, u32[]{:S(2)}) collective-permute-start(bf16[1024,256]{1,0:T(8,128)(2,1)S(1)} %collective-permute-done.1), channel_id=1, source_target_pairs={{0,4},{4,8},{8,12},{12,16},{16,20},{20,24},{24,28},{28,0},{1,5},{5... | collective-permute-start | bytes 1572872 | tf_op jit(solution)/shard_map/ppermute | solution.py:18
  165.6 11.3 %collective-permute-start.9 = (bf16[1024,256]{1,0:T(8,128)(2,1)S(1)}, bf16[1024,256]{1,0:T(8,128)(2,1)}, u32[]{:S(2)}, u32[]{:S(2)}) collective-permute-start(bf16[1024,256]{1,0:T(8,128)(2,1)S(1)} %collective-permute-done.8), channel_id=1, source_target_pairs={{0,4},{4,8},{8,12},{12,16},{16,20},{20,24},{24,28},{28,0},{1,5},{5... | collective-permute-start | bytes 1572872 | tf_op jit(solution)/shard_map/ppermute | solution.py:18
  171.2 5.7 %copy-start.5 = (bf16[1024,256]{1,0:T(8,128)(2,1)}, bf16[1024,256]{1,0:T(8,128)(2,1)S(1)}, u32[]{:S(2)}) copy-start(bf16[1024,256]{1,0:T(8,128)(2,1)S(1)} %collective-permute-done.2) | copy-start | bytes 1572868
  171.2 11.3 %collective-permute-start.3 = (bf16[1024,256]{1,0:T(8,128)(2,1)S(1)}, bf16[1024,256]{1,0:T(8,128)(2,1)}, u32[]{:S(2)}, u32[]{:S(2)}) collective-permute-start(bf16[1024,256]{1,0:T(8,128)(2,1)S(1)} %collective-permute-done.2), channel_id=1, source_target_pairs={{0,4},{4,8},{8,12},{12,16},{16,20},{20,24},{24,28},{28,0},{1,5},{5... | collective-permute-start | bytes 1572872 | tf_op jit(solution)/shard_map/ppermute | solution.py:18
  176.9 11.2 %collective-permute-start.10 = (bf16[1024,256]{1,0:T(8,128)(2,1)}, bf16[1024,256]{1,0:T(8,128)(2,1)}, u32[]{:S(2)}, u32[]{:S(2)}) collective-permute-start(bf16[1024,256]{1,0:T(8,128)(2,1)} %collective-permute-done.9), channel_id=1, source_target_pairs={{0,4},{4,8},{8,12},{12,16},{16,20},{20,24},{24,28},{28,0},{1,5},{5... | collective-permute-start | bytes 1572872 | tf_op jit(solution)/shard_map/ppermute | solution.py:18
  182.5 14.3 %collective-permute-start.4 = (bf16[1024,256]{1,0:T(8,128)(2,1)}, bf16[1024,256]{1,0:T(8,128)(2,1)}, u32[]{:S(2)}, u32[]{:S(2)}) collective-permute-start(bf16[1024,256]{1,0:T(8,128)(2,1)} %collective-permute-done.3), channel_id=1, source_target_pairs={{0,4},{4,8},{8,12},{12,16},{16,20},{20,24},{24,28},{28,0},{1,5},{5... | collective-permute-start | bytes 1572872 | tf_op jit(solution)/shard_map/ppermute | solution.py:18
  182.9 7.8 %copy-start.2 = (bf16[1024,256]{1,0:T(8,128)(2,1)S(1)}, bf16[1024,256]{1,0:T(8,128)(2,1)}, u32[]{:S(2)}) copy-start(bf16[1024,256]{1,0:T(8,128)(2,1)} %get-tuple-element.8) | copy-start | bytes 1572868
  183.4 10.7 %copy-start.1 = (bf16[1024,256]{1,0:T(8,128)(2,1)S(1)}, bf16[1024,256]{1,0:T(8,128)(2,1)}, u32[]{:S(2)}) copy-start(bf16[1024,256]{1,0:T(8,128)(2,1)} %get-tuple-element.6) | copy-start | bytes 1572868
  188.2 11.1 %collective-permute-start.11 = (bf16[1024,256]{1,0:T(8,128)(2,1)}, bf16[1024,256]{1,0:T(8,128)(2,1)S(1)}, u32[]{:S(2)}, u32[]{:S(2)}) collective-permute-start(bf16[1024,256]{1,0:T(8,128)(2,1)} %collective-permute-done.10), channel_id=1, source_target_pairs={{0,4},{4,8},{8,12},{12,16},{16,20},{20,24},{24,28},{28,0},{1,5},{5... | collective-permute-start | bytes 1572872 | tf_op jit(solution)/shard_map/ppermute | solution.py:18
  190.7 6.8 %copy-start.4 = (bf16[1024,256]{1,0:T(8,128)(2,1)S(1)}, bf16[1024,256]{1,0:T(8,128)(2,1)}, u32[]{:S(2)}) copy-start(bf16[1024,256]{1,0:T(8,128)(2,1)} %copy-done.3) | copy-start | bytes 1572868
  191.6 8.6 %copy-start.6 = (bf16[1024,256]{1,0:T(8,128)(2,1)S(1)}, bf16[1024,256]{1,0:T(8,128)(2,1)}, u32[]{:S(2)}) copy-start(bf16[1024,256]{1,0:T(8,128)(2,1)} %copy-done.5) | copy-start | bytes 1572868
  196.8 9.7 %collective-permute-start.5 = (bf16[1024,256]{1,0:T(8,128)(2,1)}, bf16[1024,256]{1,0:T(8,128)(2,1)S(1)}, u32[]{:S(2)}, u32[]{:S(2)}) collective-permute-start(bf16[1024,256]{1,0:T(8,128)(2,1)} %collective-permute-done.4), channel_id=1, source_target_pairs={{0,4},{4,8},{8,12},{12,16},{16,20},{20,24},{24,28},{28,0},{1,5},{5... | collective-permute-start | bytes 1572872 | tf_op jit(solution)/shard_map/ppermute | solution.py:18
  199.3 12.9 %collective-permute-start.12 = (bf16[1024,256]{1,0:T(8,128)(2,1)S(1)}, bf16[1024,256]{1,0:T(8,128)(2,1)S(1)}, u32[]{:S(2)}, u32[]{:S(2)}) collective-permute-start(bf16[1024,256]{1,0:T(8,128)(2,1)S(1)} %collective-permute-done.11), channel_id=1, source_target_pairs={{0,4},{4,8},{8,12},{12,16},{16,20},{20,24},{24,28},{28,0},{1,5},{5... | collective-permute-start | bytes 1572872 | tf_op jit(solution)/shard_map/ppermute | solution.py:18
  206.5 11.2 %collective-permute-start.6 = (bf16[1024,256]{1,0:T(8,128)(2,1)S(1)}, bf16[1024,256]{1,0:T(8,128)(2,1)S(1)}, u32[]{:S(2)}, u32[]{:S(2)}) collective-permute-start(bf16[1024,256]{1,0:T(8,128)(2,1)S(1)} %collective-permute-done.5), channel_id=1, source_target_pairs={{0,4},{4,8},{8,12},{12,16},{16,20},{20,24},{24,28},{28,0},{1,5},{5... | collective-permute-start | bytes 1572872 | tf_op jit(solution)/shard_map/ppermute | solution.py:18
  212.1 11.2 %collective-permute-start.13 = (bf16[1024,256]{1,0:T(8,128)(2,1)S(1)}, bf16[1024,256]{1,0:T(8,128)(2,1)S(1)}, u32[]{:S(2)}, u32[]{:S(2)}) collective-permute-start(bf16[1024,256]{1,0:T(8,128)(2,1)S(1)} %collective-permute-done.12), channel_id=1, source_target_pairs={{0,4},{4,8},{8,12},{12,16},{16,20},{20,24},{24,28},{28,0},{1,5},{5... | collective-permute-start | bytes 1572872 | tf_op jit(solution)/shard_map/ppermute | solution.py:18
  (3 other events, 15.2 us)
Sparse Core Ops, SparseCore 0:
  15.2 123.8 all-reduce.2
Sparse Core Ops, SparseCore 1:
  17.4 39.9 all-gather.1
